TPU v7x, 256 devices: a whole 4x4x8 slice. The times are simulated.
256 devices in a mesh: seq: 8 (over y, core), users: 32 (over x, z).
Axes of the slice: x: 4, y: 4, z: 8, core: 2. Of those that a mesh axis runs over, the one named last changes fastest.
Arguments:
- hidden: float32 [32, 8192, 512], P('users', 'seq'), may hold values from -256 to 256
- target: bfloat16 [32, 8192, 512], P('users', 'seq'), may hold values from -0.25 to 0.25
- pool_table: bfloat16 [8192, 512], P('users'), may hold values from -1 to 1
- pool_items: int32 [8192], P('users'), may hold values from 1 to 16383
- labels: int32 [32, 8192], P('users', 'seq'), may hold values from 1 to 16383
- chosen: int32 [32, 64, 8], P('users', 'seq'), may hold values from 0 to 31, all different within a row
- offsets: int32 [32, 5], P('users'), may hold values from 0 to 8192, as said below
Outputs:
- loss: float32 [], replicated
- grad_hidden: float32 [32, 8192, 512], P('users', 'seq')
- grad_table: float32 [8192, 512], P('users')
Inputs may be any that keep to these rules, and one draw needn't show every extreme that they name: Each row offsets[u] starts at 0 and rises strictly; its last entry is the number of live positions of group u, and equals 8192 in some group; positions from it on are padding. `chosen`: each position block names 8 different negative blocks.
All inputs are finite; a program needn't handle non-finite values.
Results may differ from a plain program's by a relative error of at most 0.003.
Values may be sent and summed in bfloat16 or wider, within the bound.
A program may use at most 192 MiB of HBM per device.

v0:
```python
import jax
import jax.numpy as jnp
from jax import lax
from jax.sharding import PartitionSpec as P

NB = 256
PB = 128


def history_weights(bounds, positions):
    starts = bounds[:-1]
    finish = bounds[1:]
    lengths = (finish - starts).astype(jnp.float32)
    inside = (positions[..., None] >= starts) & (positions[..., None] < finish)
    return jnp.sum(jnp.where(inside, 1.0 / lengths, 0.0), axis=-1)


def block_terms(states, target, labels, weights, chosen, pool_rows, pool_ids, factor):
    narrow = states.astype(jnp.bfloat16)
    negatives = jnp.take(pool_rows, chosen, axis=0).reshape(-1, pool_rows.shape[2])
    neg_items = jnp.take(pool_ids, chosen, axis=0).reshape(-1)
    scores = jnp.dot(narrow, negatives.T, preferred_element_type=jnp.float32)
    target_wide = target.astype(jnp.float32)
    positive = jnp.sum(narrow.astype(jnp.float32) * target_wide, axis=1)
    masked = jnp.where(neg_items[None, :] == labels[:, None], -1e30, scores)
    peak = jnp.maximum(positive, jnp.max(masked, axis=1))
    neg_exp = jnp.exp(masked - peak[:, None])
    pos_exp = jnp.exp(positive - peak)
    totals = pos_exp + jnp.sum(neg_exp, axis=1)
    cross = peak + jnp.log(totals) - positive
    coeff = weights * factor
    neg_grad = (coeff[:, None] * neg_exp / totals[:, None]).astype(jnp.bfloat16)
    pos_grad = coeff * (pos_exp / totals - 1.0)
    state_grad = (
        jnp.dot(neg_grad, negatives, preferred_element_type=jnp.float32)
        + pos_grad[:, None] * target_wide
    )
    pool_grad = jnp.dot(neg_grad.T, narrow, preferred_element_type=jnp.float32)
    pool_grad = pool_grad.reshape(chosen.shape[0], pool_rows.shape[1], pool_rows.shape[2])
    return (jnp.sum(weights * cross), state_grad, pool_grad)


def run_blocks(
    states,
    targets,
    label_rows,
    weights,
    picked,
    visit_order,
    live_count,
    pool_rows,
    pool_ids,
    factor,
):
    batched = jax.vmap(block_terms, in_axes=(0, 0, 0, 0, 0, None, None, None))
    rounds = (live_count + 3) // 4

    def advance(turn_index, carried):
        loss_acc, grad_acc, state_acc = carried
        slot_picks = lax.dynamic_slice_in_dim(visit_order, turn_index * 4, 4)
        picked_now = jnp.take(picked, slot_picks, axis=0)
        part_loss, state_grad, pool_grad = batched(
            jnp.take(states, slot_picks, axis=0),
            jnp.take(targets, slot_picks, axis=0),
            jnp.take(label_rows, slot_picks, axis=0),
            jnp.take(weights, slot_picks, axis=0),
            picked_now,
            pool_rows,
            pool_ids,
            factor,
        )
        grad_acc = grad_acc.at[picked_now.reshape(-1)].add(
            pool_grad.reshape((-1,) + pool_grad.shape[2:])
        )
        state_acc = state_acc.at[slot_picks].set(state_grad)
        return (loss_acc + jnp.sum(part_loss), grad_acc, state_acc)

    initial = (
        jnp.zeros((), jnp.float32),
        jnp.zeros(pool_rows.shape, jnp.float32),
        jnp.zeros(states.shape, jnp.float32),
    )
    return lax.fori_loop(0, rounds, advance, initial)


def per_device(hidden, target, pool_table, pool_items, labels, chosen, offsets):
    user_count = lax.axis_size("users")
    length = hidden.shape[1]
    features = hidden.shape[2]
    block_count = length // PB
    shard_rows, shard_items = (
        lax.all_gather(pool_table, "users", axis=0, tiled=True),
        lax.all_gather(pool_items, "users", axis=0, tiled=True),
    )
    pool_rows = shard_rows.reshape(-1, NB, features)
    pool_ids = shard_items.reshape(-1, NB)
    factor = 1.0 / (user_count * (offsets.shape[1] - 1))
    seq_place = lax.axis_index("seq")
    live_blocks = (offsets[0, -1] + PB - 1) // PB
    states = hidden.reshape(block_count, PB, features)
    targets = target.reshape(block_count, PB, features)
    label_rows = labels.reshape(block_count, PB)
    picked = chosen.reshape(block_count, chosen.shape[2])
    within = jnp.arange(PB, dtype=jnp.int32)
    slot_index = jnp.arange(block_count, dtype=jnp.int32)
    positions = seq_place * length + slot_index[:, None] * PB + within[None, :]
    weights = history_weights(offsets[0], positions)
    live_count = jnp.clip(live_blocks - seq_place * block_count, 0, block_count)
    loss_part, grad_pool, state_grad = run_blocks(
        states,
        targets,
        label_rows,
        weights,
        picked,
        slot_index,
        live_count,
        pool_rows,
        pool_ids,
        factor,
    )
    grad_hidden = state_grad.reshape(hidden.shape)
    loss_total = lax.psum(loss_part, ("seq", "users")) * factor
    grad_full = grad_pool.reshape(-1, features)
    owned_rows = lax.psum_scatter(grad_full, "users", scatter_dimension=0, tiled=True)
    grad_table = lax.psum(owned_rows, "seq")
    return (loss_total, grad_hidden, grad_table)


def solution(mesh):
    return jax.shard_map(
        per_device,
        mesh=mesh,
        in_specs=(
            P("users", "seq", None),
            P("users", "seq", None),
            P("users", None),
            P("users"),
            P("users", "seq"),
            P("users", "seq", None),
            P("users", None),
        ),
        out_specs=(P(), P("users", "seq", None), P("users", None)),
        check_vma=False,
    )
```

profile of v0, /device:TPU:1, one launch (start us, length us, event | category | flops | bytes accessed | tf_op | source)
XLA Modules:
  0.0 615.0 jit_solution(12936901382694185869)
XLA Ops:
  9.9 38.2 %all-gather = s32[32,1,256]{2,1,0:T(1,128)S(1)} all-gather(s32[1,1,256]{2,1,0:T(1,128)} %bitcast.72), channel_id=1, replica_groups=mesh['seq'=8,'users'=32] {'users'}, dimensions={0}, use_global_device_ids=true | all-gather | bytes 33792 | tf_op jit(solution)/shard_map/all_gather | solution.py:93
  51.7 59.8 %all-gather.3.cloned.1.call-done = bf16[8192,512]{1,0:T(8,128)(2,1)} async-done(((bf16[256,512]{1,0:T(8,128)(2,1)}), bf16[8192,512]{1,0:T(8,128)(2,1)}) %all-gather.3.cloned.1.call-update) | async-done | bytes 8388624 | tf_op jit(solution)/shard_map/all_gather | solution.py:92
  113.1 7.9 %broadcast_in_dim.126 = f32[32,256,512]{2,1,0:T(8,128)} broadcast(f32[]{:T(128)} %copy.36), dimensions={} | broadcast | bytes 16777220 | tf_op jit(solution)/shard_map/broadcast_in_dim | solution.py:80
  120.9 164.0 %while.16 = (s32[]{:T(128)}, f32[]{:T(128)}, f32[32,256,512]{2,1,0:T(8,128)}, f32[8,128,512]{2,1,0:T(8,128)}, s32[]{:T(128)}, /*index=5*/s32[8]{0:T(128)S(1)}, f...) while((s32[]{:T(128)}, f32[]{:T(128)}, ...), condition=%wide.region_8.9_spmd, body=%wide.region_1.8_spmd.sunk | while | flops 3252174336 | bytes 194429456 | solution.py:83
  123.9 1.8 gather_fusion
  126.6 8.4 %gather_fusion.5 = bf16[32,256,512]{2,1,0:T(8,128)(2,1)} fusion(bf16[32,256,512]{2,1,0:T(8,128)(2,1)} %get-tuple-element.362, s32[1024]{0:T(1024)S(1)} %pad_clamp_fusion.5), kind=kCustom, calls=%fused_computation.6.clone.1 | custom fusion | bytes 16777344 | tf_op jit(solution)/shard_map/while/body/vmap(jit(_take))/gather | solution.py:20
  135.0 4.7 bitcast_select_fusion.3
  139.7 2.8 fusion.24
  142.9 1.9 copy-done
  147.0 6.5 %convolution_add_fusion.2 = f32[4,128,512]{2,1,0:T(8,128)S(1)} fusion(bf16[4,2048,512]{2,1,0:T(8,128)(2,1)} %copy-done.1, f32[4,128]{1,0:T(4,128)S(1)} %get-tuple-element.315, bf16[4,128,512]{2,1,0:T(8,128)(2,1)S(1)} %gather_fusion, pred[4]{0:T(512)(128)(4,1)S(1)} %get-tuple-element.305, f32[4,128,2048]{2,1,0:T(8,128)} %copy-done, ...), kind=kOutput, calls=%fused_computation.17.clone.1 | convolution fusion | flops 1081081856 | bytes 14198788 | tf_op jit(solution)/shard_map/while/body/vmap()/dot_general | solution.py:35
  153.5 2.8 scatter_fusion.1
  156.3 10.4 %fusion.27 = f32[4,2048,512]{2,1,0:T(8,128)} fusion(bf16[4,128,512]{2,1,0:T(8,128)(2,1)S(1)} %get-tuple-element.308, f32[4,128,2048]{2,1,0:T(8,128)} %copy-done, f32[4,128]{1,0:T(4,128)S(1)} %get-tuple-element.313, f32[4,128]{1,0:T(4,128)S(1)} %get-tuple-element.314, f32[4,128]{1,0:T(4,128)S(1)} %max.31, s32[4,128]{1,0:T(4,128)S(1)} %broadcast_select_fusion.7, ...), kind=kOutput, calls=%fused_computation.40.clone.1 | convolution fusion | flops 1080033280 | bytes 21536768 | tf_op jit(solution)/shard_map/while/body/vmap()/dot_general | solution.py:38
  166.7 36.3 %scatter_fusion = f32[32,256,512]{2,1,0:T(8,128)} fusion(f32[32,256,512]{2,1,0:T(8,128)} %get-tuple-element.335, s32[32]{0:T(128)S(1)} %fusion.26, f32[32,256,512]{2,1,0:T(8,128)} %bitcast.60), kind=kCustom, calls=%fused_computation.7.clone.1 | custom fusion | flops 4194304 | bytes 50331776 | tf_op jit(solution)/shard_map/while/body/scatter-add | solution.py:72
  208.6 8.4 %gather_fusion.5 = bf16[32,256,512]{2,1,0:T(8,128)(2,1)} fusion(bf16[32,256,512]{2,1,0:T(8,128)(2,1)} %get-tuple-element.362, s32[1024]{0:T(1024)S(1)} %pad_clamp_fusion.5), kind=kCustom, calls=%fused_computation.6.clone.1 | custom fusion | bytes 16777344 | tf_op jit(solution)/shard_map/while/body/vmap(jit(_take))/gather | solution.py:20
  217.0 4.7 bitcast_select_fusion.3
  221.7 2.9 fusion.24
  224.9 1.9 copy-done
  229.0 6.5 %convolution_add_fusion.2 = f32[4,128,512]{2,1,0:T(8,128)S(1)} fusion(bf16[4,2048,512]{2,1,0:T(8,128)(2,1)} %copy-done.1, f32[4,128]{1,0:T(4,128)S(1)} %get-tuple-element.315, bf16[4,128,512]{2,1,0:T(8,128)(2,1)S(1)} %gather_fusion, pred[4]{0:T(512)(128)(4,1)S(1)} %get-tuple-element.305, f32[4,128,2048]{2,1,0:T(8,128)} %copy-done, ...), kind=kOutput, calls=%fused_computation.17.clone.1 | convolution fusion | flops 1081081856 | bytes 14198788 | tf_op jit(solution)/shard_map/while/body/vmap()/dot_general | solution.py:35
  235.5 2.8 scatter_fusion.1
  238.2 10.4 %fusion.27 = f32[4,2048,512]{2,1,0:T(8,128)} fusion(bf16[4,128,512]{2,1,0:T(8,128)(2,1)S(1)} %get-tuple-element.308, f32[4,128,2048]{2,1,0:T(8,128)} %copy-done, f32[4,128]{1,0:T(4,128)S(1)} %get-tuple-element.313, f32[4,128]{1,0:T(4,128)S(1)} %get-tuple-element.314, f32[4,128]{1,0:T(4,128)S(1)} %max.31, s32[4,128]{1,0:T(4,128)S(1)} %broadcast_select_fusion.7, ...), kind=kOutput, calls=%fused_computation.40.clone.1 | convolution fusion | flops 1080033280 | bytes 21536768 | tf_op jit(solution)/shard_map/while/body/vmap()/dot_general | solution.py:38
  248.7 36.2 %scatter_fusion = f32[32,256,512]{2,1,0:T(8,128)} fusion(f32[32,256,512]{2,1,0:T(8,128)} %get-tuple-element.335, s32[32]{0:T(128)S(1)} %fusion.26, f32[32,256,512]{2,1,0:T(8,128)} %bitcast.60), kind=kCustom, calls=%fused_computation.7.clone.1 | custom fusion | flops 4194304 | bytes 50331776 | tf_op jit(solution)/shard_map/while/body/scatter-add | solution.py:72
  285.0 240.3 %reduce-scatter.2.cloned.1.call-done = f32[256,512]{1,0:T(8,128)} async-done(((f32[8192,512]{1,0:T(8,128)}), f32[256,512]{1,0:T(8,128)}) %reduce-scatter.2.cloned.1.call-update) | async-done | bytes 524304 | tf_op jit(solution)/shard_map/reduce_scatter | solution.py:124
  525.3 79.5 %psum.14 = f32[]{:T(128)} all-reduce(f32[]{:T(128)} %get-tuple-element.169), channel_id=1, replica_groups=mesh['seq'=8,'users'=32] {'seq','users'}, use_global_device_ids=true, to_apply=%region_9.10 | all-reduce | flops 1 | bytes 8 | tf_op jit(solution)/shard_map/psum | solution.py:122
  605.5 1.9 copy.37
  (72 shorter events, 20.7 us)
Async XLA Ops:
  7.2 104.3 %all-gather.3.cloned.1.call-start = ((), (), s32[]{:S(2)}) async-start(), calls=%async_computation.1 | async-start | bytes 8650752 | tf_op jit(solution)/shard_map/all_gather | solution.py:92
  7.9 517.4 %reduce-scatter.2.cloned.1.call-start = ((), (), s32[]{:S(2)}) async-start(), calls=%async_computation.2 | async-start | bytes 17301504 | tf_op jit(solution)/shard_map/reduce_scatter | solution.py:124
  113.1 7.9 %copy-start.2 = (s32[1,8,8]{2,1,0:T(8,128)S(1)}, s32[1,8,8]{2,1,0:T(8,128)}, u32[]{:S(2)}) copy-start(s32[1,8,8]{2,1,0:T(8,128)} %param.14) | copy-start | bytes 772
  113.1 7.9 %copy-start.3 = (s32[1,1024]{1,0:T(1,128)S(1)}, s32[1,1024]{1,0:T(1,128)}, u32[]{:S(2)}) copy-start(s32[1,1024]{1,0:T(1,128)} %param.13) | copy-start | bytes 12292
  139.7 3.2 copy-start.1
  142.9 1.9 copy-start
  221.7 3.2 copy-start.1
  224.9 1.9 copy-start
  284.9 320.6 %all-reduce.2.cloned.1.call-start = ((), (), s32[]{:S(2)}) async-start(), calls=%async_computation.3 | async-start | bytes 1048576 | tf_op jit(solution)/shard_map/psum | solution.py:125
Sparse Core Ops, SparseCore 0:
  10.6 100.8 all-gather.2
  285.0 240.2 reduce-scatter.1
  527.6 66.9 all-reduce.1
where the time goes:
time: 616 us; the launch traced here: 615 us
  waiting for transfers between devices  301 us (49%)
  blocking collectives  118 us (19%)
  other arithmetic  89.2 us (14%)
  local copies, waits for them, and re-layouts  50.1 us (8%)
  matrix products  39.5 us (6%)
  between operations  16.2 us (3%)
    reduce_scatter x1, waiting for transfers between devices, per_device(): lax.psum_scatter(grad_full, 'users', scatter_dimension=0, tiled=True)  240 us
    psum x1, blocking collectives, per_device(): loss_total = lax.psum(loss_part, ('seq', 'users')) * factor  79.5 us
    scatter-add x2, other arithmetic, advance(): grad_acc.at[picked_now.reshape(-1)]  72.5 us
    all_gather x1, waiting for transfers between devices, per_device(): lax.all_gather(pool_table, 'users', axis=0, tiled=True)  59.8 us
    all_gather x1, blocking collectives, per_device(): lax.all_gather(pool_items, 'users', axis=0, tiled=True)  38.2 us
    dot_general x2, matrix products, block_terms(): pool_grad = jnp.dot(neg_grad.T, narrow, preferred_element_type=jnp.float32)  20.9 us
    gather x2, local copies, waits for them, and re-layouts, block_terms(): jnp.take(pool_rows, chosen, axis=0).reshape(-1, pool_rows.shape[2])  16.8 us
    dot_general x2, matrix products, block_terms(): jnp.dot(neg_grad, negatives, preferred_element_type=jnp.float32)  12.9 us
  transfers between devices with their start and end apart: 3, of which 2 were waited for; matrix products, arithmetic and copies ran while one was open for 1% of the time, Pallas kernels for 0%

commit v1 on v0

--- a/solution.py
+++ b/solution.py
@@ -90,7 +90,9 @@
     block_count = length // PB
     shard_rows, shard_items = (
         lax.all_gather(pool_table, "users", axis=0, tiled=True),
-        lax.all_gather(pool_items, "users", axis=0, tiled=True),
+        jnp.concatenate(
+            lax.all_to_all(jnp.stack([pool_items] * lax.axis_size("users")), "users", 0, 0), axis=0
+        ),
     )
     pool_rows = shard_rows.reshape(-1, NB, features)
     pool_ids = shard_items.reshape(-1, NB)

time: 616 us -> 617 us (level)
  blocking collectives: 118 us -> 79.7 us
  waiting for transfers between devices: 301 us -> 327 us
  starting transfers between devices: 0.12 us -> 12 us
    all_gather x1 -> x0, blocking collectives: 38.2 us -> none  [per_device(): lax.all_gather(pool_items, 'users', axis=0, tiled=True)]
    all_gather x1, waiting for transfers between devices: 59.8 us -> 81.6 us  [per_device(): lax.all_gather(pool_table, 'users', axis=0, tiled=True)]
    all_to_all x0 -> x1, starting transfers between devices: none -> 11.9 us  [per_device(): lax.all_to_all(jnp.stack([pool_items] * lax.axis_size('users')), 'users',...]
  transfers between devices with their start and end apart: 3 -> 4, of which waited for: 2 -> 3; matrix products, arithmetic and copies ran while one was open for 1% -> 1% of each run, Pallas kernels for 0% -> 0%
where the time goes in v1:
time: 617 us; the launch traced here: 616 us
  waiting for transfers between devices  327 us (53%)
  other arithmetic  89.2 us (14%)
  blocking collectives  79.7 us (13%)
  local copies, waits for them, and re-layouts  51.4 us (8%)
  matrix products  39.5 us (6%)
  between operations  16.3 us (3%)
  starting transfers between devices  12 us (2%)
    reduce_scatter x1, waiting for transfers between devices, per_device(): lax.psum_scatter(grad_full, 'users', scatter_dimension=0, tiled=True)  241 us
    all_gather x1, waiting for transfers between devices, per_device(): lax.all_gather(pool_table, 'users', axis=0, tiled=True)  81.6 us
    psum x1, blocking collectives, per_device(): loss_total = lax.psum(loss_part, ('seq', 'users')) * factor  79.7 us
    scatter-add x2, other arithmetic, advance(): grad_acc.at[picked_now.reshape(-1)]  72.5 us
    dot_general x2, matrix products, block_terms(): pool_grad = jnp.dot(neg_grad.T, narrow, preferred_element_type=jnp.float32)  20.9 us
    gather x2, local copies, waits for them, and re-layouts, block_terms(): jnp.take(pool_rows, chosen, axis=0).reshape(-1, pool_rows.shape[2])  16.8 us
    dot_general x2, matrix products, block_terms(): jnp.dot(neg_grad, negatives, preferred_element_type=jnp.float32)  12.9 us
  transfers between devices with their start and end apart: 4, of which 3 were waited for; matrix products, arithmetic and copies ran while one was open for 1% of the time, Pallas kernels for 0%

profile of v1, /device:TPU:1, one launch (start us, length us, event | category | flops | bytes accessed | tf_op | source)
XLA Modules:
  0.0 616.1 jit_solution(3176089327698085235)
XLA Ops:
  9.2 11.9 %all-to-all-start = ((s32[32,1,256]{2,1,0:T(1,128)}), s32[32,1,256]{2,1,0:T(1,128)S(1)}, u32[]{:S(2)}, u32[]{:S(2)}) async-start(s32[32,1,256]{2,1,0:T(1,128)} %stack.2), calls=%async_computation | async-start | bytes 65536 | tf_op jit(solution)/shard_map/all_to_all | solution.py:94
  26.6 3.3 all-to-all-done
  29.8 81.6 %all-gather.2.cloned.1.call-done = bf16[8192,512]{1,0:T(8,128)(2,1)} async-done(((bf16[256,512]{1,0:T(8,128)(2,1)}), bf16[8192,512]{1,0:T(8,128)(2,1)}) %all-gather.2.cloned.1.call-update) | async-done | bytes 8388624 | tf_op jit(solution)/shard_map/all_gather | solution.py:92
  113.0 7.9 %broadcast_in_dim.126 = f32[32,256,512]{2,1,0:T(8,128)} broadcast(f32[]{:T(128)} %copy.36), dimensions={} | broadcast | bytes 16777220 | tf_op jit(solution)/shard_map/broadcast_in_dim | solution.py:80
  120.9 164.2 %while.16 = (s32[]{:T(128)}, f32[]{:T(128)}, f32[32,256,512]{2,1,0:T(8,128)}, f32[8,128,512]{2,1,0:T(8,128)}, s32[]{:T(128)}, /*index=5*/s32[8]{0:T(128)S(1)}, f...) while((s32[]{:T(128)}, f32[]{:T(128)}, ...), condition=%wide.region_8.9_spmd, body=%wide.region_1.8_spmd.sunk | while | flops 3252174336 | bytes 194429456 | solution.py:83
  126.6 8.4 %gather_fusion.5 = bf16[32,256,512]{2,1,0:T(8,128)(2,1)} fusion(bf16[32,256,512]{2,1,0:T(8,128)(2,1)} %get-tuple-element.362, s32[1024]{0:T(1024)S(1)} %pad_clamp_fusion.5), kind=kCustom, calls=%fused_computation.6.clone.1 | custom fusion | bytes 16777344 | tf_op jit(solution)/shard_map/while/body/vmap(jit(_take))/gather | solution.py:20
  135.0 4.7 bitcast_select_fusion.3
  139.7 2.8 fusion.24
  142.9 1.9 copy-done
  147.1 6.5 %convolution_add_fusion.2 = f32[4,128,512]{2,1,0:T(8,128)S(1)} fusion(bf16[4,2048,512]{2,1,0:T(8,128)(2,1)} %copy-done.1, f32[4,128]{1,0:T(4,128)S(1)} %get-tuple-element.315, bf16[4,128,512]{2,1,0:T(8,128)(2,1)S(1)} %gather_fusion, pred[4]{0:T(512)(128)(4,1)S(1)} %get-tuple-element.305, f32[4,128,2048]{2,1,0:T(8,128)} %copy-done, ...), kind=kOutput, calls=%fused_computation.17.clone.1 | convolution fusion | flops 1081081856 | bytes 14198788 | tf_op jit(solution)/shard_map/while/body/vmap()/dot_general | solution.py:35
  153.6 2.8 scatter_fusion.1
  156.3 10.4 %fusion.27 = f32[4,2048,512]{2,1,0:T(8,128)} fusion(bf16[4,128,512]{2,1,0:T(8,128)(2,1)S(1)} %get-tuple-element.308, f32[4,128,2048]{2,1,0:T(8,128)} %copy-done, f32[4,128]{1,0:T(4,128)S(1)} %get-tuple-element.313, f32[4,128]{1,0:T(4,128)S(1)} %get-tuple-element.314, f32[4,128]{1,0:T(4,128)S(1)} %max.31, s32[4,128]{1,0:T(4,128)S(1)} %broadcast_select_fusion.7, ...), kind=kOutput, calls=%fused_computation.40.clone.1 | convolution fusion | flops 1080033280 | bytes 21536768 | tf_op jit(solution)/shard_map/while/body/vmap()/dot_general | solution.py:38
  166.8 36.3 %scatter_fusion = f32[32,256,512]{2,1,0:T(8,128)} fusion(f32[32,256,512]{2,1,0:T(8,128)} %get-tuple-element.335, s32[32]{0:T(128)S(1)} %fusion.26, f32[32,256,512]{2,1,0:T(8,128)} %bitcast.59), kind=kCustom, calls=%fused_computation.7.clone.1 | custom fusion | flops 4194304 | bytes 50331776 | tf_op jit(solution)/shard_map/while/body/scatter-add | solution.py:72
  208.7 8.4 %gather_fusion.5 = bf16[32,256,512]{2,1,0:T(8,128)(2,1)} fusion(bf16[32,256,512]{2,1,0:T(8,128)(2,1)} %get-tuple-element.362, s32[1024]{0:T(1024)S(1)} %pad_clamp_fusion.5), kind=kCustom, calls=%fused_computation.6.clone.1 | custom fusion | bytes 16777344 | tf_op jit(solution)/shard_map/while/body/vmap(jit(_take))/gather | solution.py:20
  217.1 4.7 bitcast_select_fusion.3
  221.8 2.8 fusion.24
  225.0 1.9 copy-done
  229.2 6.5 %convolution_add_fusion.2 = f32[4,128,512]{2,1,0:T(8,128)S(1)} fusion(bf16[4,2048,512]{2,1,0:T(8,128)(2,1)} %copy-done.1, f32[4,128]{1,0:T(4,128)S(1)} %get-tuple-element.315, bf16[4,128,512]{2,1,0:T(8,128)(2,1)S(1)} %gather_fusion, pred[4]{0:T(512)(128)(4,1)S(1)} %get-tuple-element.305, f32[4,128,2048]{2,1,0:T(8,128)} %copy-done, ...), kind=kOutput, calls=%fused_computation.17.clone.1 | convolution fusion | flops 1081081856 | bytes 14198788 | tf_op jit(solution)/shard_map/while/body/vmap()/dot_general | solution.py:35
  235.7 2.8 scatter_fusion.1
  238.4 10.4 %fusion.27 = f32[4,2048,512]{2,1,0:T(8,128)} fusion(bf16[4,128,512]{2,1,0:T(8,128)(2,1)S(1)} %get-tuple-element.308, f32[4,128,2048]{2,1,0:T(8,128)} %copy-done, f32[4,128]{1,0:T(4,128)S(1)} %get-tuple-element.313, f32[4,128]{1,0:T(4,128)S(1)} %get-tuple-element.314, f32[4,128]{1,0:T(4,128)S(1)} %max.31, s32[4,128]{1,0:T(4,128)S(1)} %broadcast_select_fusion.7, ...), kind=kOutput, calls=%fused_computation.40.clone.1 | convolution fusion | flops 1080033280 | bytes 21536768 | tf_op jit(solution)/shard_map/while/body/vmap()/dot_general | solution.py:38
  248.9 36.2 %scatter_fusion = f32[32,256,512]{2,1,0:T(8,128)} fusion(f32[32,256,512]{2,1,0:T(8,128)} %get-tuple-element.335, s32[32]{0:T(128)S(1)} %fusion.26, f32[32,256,512]{2,1,0:T(8,128)} %bitcast.59), kind=kCustom, calls=%fused_computation.7.clone.1 | custom fusion | flops 4194304 | bytes 50331776 | tf_op jit(solution)/shard_map/while/body/scatter-add | solution.py:72
  285.2 241.0 %reduce-scatter.2.cloned.1.call-done = f32[256,512]{1,0:T(8,128)} async-done(((f32[8192,512]{1,0:T(8,128)}), f32[256,512]{1,0:T(8,128)}) %reduce-scatter.2.cloned.1.call-update) | async-done | bytes 524304 | tf_op jit(solution)/shard_map/reduce_scatter | solution.py:126
  526.2 79.7 %psum.14 = f32[]{:T(128)} all-reduce(f32[]{:T(128)} %get-tuple-element.169), channel_id=1, replica_groups=mesh['seq'=8,'users'=32] {'seq','users'}, use_global_device_ids=true, to_apply=%region_9.10 | all-reduce | flops 1 | bytes 8 | tf_op jit(solution)/shard_map/psum | solution.py:124
  606.6 1.9 copy.37
  (74 shorter events, 23.8 us)
Async XLA Ops:
  7.2 104.3 %all-gather.2.cloned.1.call-start = ((), (), s32[]{:S(2)}) async-start(), calls=%async_computation.2 | async-start | bytes 8650752 | tf_op jit(solution)/shard_map/all_gather | solution.py:92
  9.2 20.6 %all-to-all-start = ((s32[32,1,256]{2,1,0:T(1,128)}), s32[32,1,256]{2,1,0:T(1,128)S(1)}, u32[]{:S(2)}, u32[]{:S(2)}) async-start(s32[32,1,256]{2,1,0:T(1,128)} %stack.2), calls=%async_computation | async-start | bytes 65536 | tf_op jit(solution)/shard_map/all_to_all | solution.py:94
  21.1 505.1 %reduce-scatter.2.cloned.1.call-start = ((), (), s32[]{:S(2)}) async-start(), calls=%async_computation.3 | async-start | bytes 17301504 | tf_op jit(solution)/shard_map/reduce_scatter | solution.py:126
  113.0 7.9 %copy-start.2 = (s32[1,8,8]{2,1,0:T(8,128)S(1)}, s32[1,8,8]{2,1,0:T(8,128)}, u32[]{:S(2)}) copy-start(s32[1,8,8]{2,1,0:T(8,128)} %param.14) | copy-start | bytes 772
  113.0 7.9 %copy-start.3 = (s32[1,1024]{1,0:T(1,128)S(1)}, s32[1,1024]{1,0:T(1,128)}, u32[]{:S(2)}) copy-start(s32[1,1024]{1,0:T(1,128)} %param.13) | copy-start | bytes 12292
  139.7 3.2 copy-start.1
  142.9 1.9 copy-start
  221.8 3.2 copy-start.1
  225.0 1.9 copy-start
  285.1 321.4 %all-reduce.2.cloned.1.call-start = ((), (), s32[]{:S(2)}) async-start(), calls=%async_computation.4 | async-start | bytes 1048576 | tf_op jit(solution)/shard_map/psum | solution.py:127
Sparse Core Ops, SparseCore 0:
  10.6 100.8 all-gather.1
  285.2 240.8 reduce-scatter.1
  528.5 66.9 all-reduce.1
